TPU v7x, 256 devices: a whole 4x4x8 slice. The times are simulated.
256 devices in a mesh: strat: 32 (over z, y_hi, core), grp: 8 (over x, y_lo).
Axes of the slice: x: 4, y: 4 (y_hi: 2, y_lo: 2; y = y_hi * 2 + y_lo), z: 8, core: 2. Of those that a mesh axis runs over, the one named last changes fastest.
Arguments:
- user_factors: float32 [262144, 256], P(('strat', 'grp')), may hold values from -1.5 to 1.5
- item_factors: float32 [131072, 256], P('strat'), may hold values from -1.5 to 1.5
- tile_coords: int32 [32, 8, 3, 2, 16], P('strat', 'grp'), may hold values from 0 to 31, as said below
- tile_counts: int32 [32, 8, 3], P('strat', 'grp'), may hold values from 5 to 16, as said below
- tile_values: bfloat16 [32, 8, 3, 16, 128, 128], P('strat', 'grp'), may hold values from 0 to 10
Outputs:
- users_out: float32 [262144, 256], P(('strat', 'grp'))
- items_out: float32 [131072, 256], P('strat')
Inputs may be any that keep to these rules, and one draw needn't show every extreme that they name: `tile_coords`: each list names distinct tiles; user tiles lie below 8 and item tiles below 32; entries at and after the count are ignored. `tile_counts`: in every sub-epoch some device has exactly 16 live tiles.
All inputs are finite; a program needn't handle non-finite values.
Results may differ from a plain program's by a relative error of at most 0.0018.
Values sent between devices are 32-bit elements; how exact they have to be, the bound alone decides.
A program may use at most 64 MiB of HBM per device.

v0:
```python
import jax
import jax.numpy as jnp
from jax import lax
from jax.sharding import PartitionSpec as P


def from_behind(block, axis, distance):
    devices = range(lax.axis_size(axis))
    route = [((i - distance) % len(devices), i) for i in devices]
    return lax.ppermute(block, axis, route)


def tile_terms(user_b, slab_b, coords, count, values):
    high = lax.Precision.HIGHEST
    side = values.shape[-1]
    width = user_b.shape[1]
    user_tiles = user_b.shape[0] // side
    item_tiles = slab_b.shape[0] // side
    urows = jnp.take(user_b.reshape(user_tiles, side, width), coords[0], axis=0)
    irows = jnp.take(slab_b.reshape(item_tiles, side, width), coords[1], axis=0)
    predicted = jnp.einsum("nrk,nck->nrc", urows, irows, preferred_element_type=jnp.float32)
    resid = (values.astype(jnp.float32) - predicted).astype(jnp.bfloat16)
    user_part = jnp.einsum("nrc,nck->nrk", resid, irows, preferred_element_type=jnp.float32)
    item_part = jnp.einsum("nrc,nrk->nck", resid, urows, preferred_element_type=jnp.float32)
    live = jnp.arange(coords.shape[1]) < count
    one_user = ((coords[0][:, None] == jnp.arange(user_tiles)[None, :]) & live[:, None]).astype(
        jnp.float32
    )
    one_item = ((coords[1][:, None] == jnp.arange(item_tiles)[None, :]) & live[:, None]).astype(
        jnp.float32
    )
    user_grad = jnp.einsum("nt,nrk->trk", one_user, user_part, precision=high).reshape(-1, width)
    item_grad = jnp.einsum("nt,nrk->trk", one_item, item_part, precision=high).reshape(-1, width)
    return (user_grad, item_grad)


def per_device(user_factors, item_factors, tile_coords, tile_counts, tile_values):
    users = user_factors
    slab = item_factors
    coords = tile_coords[0, 0]
    counts = tile_counts[0, 0]
    values = tile_values[0, 0]
    rounds = coords.shape[0]
    for sub in range(rounds):
        user_grad, item_grad = tile_terms(
            users.astype(jnp.bfloat16),
            slab.astype(jnp.bfloat16),
            coords[sub],
            counts[sub],
            values[sub],
        )
        users = users - 0.003 * (0.05 * users - user_grad)
        total = lax.psum(item_grad, "grp")
        slab = slab - 0.003 * (0.05 * slab - total)
        if sub + 1 < rounds:
            slab = from_behind(slab, "strat", -1)
    return (users, slab)


def solution(mesh):
    placed = (
        P(("strat", "grp"), None),
        P("strat", None),
        P("strat", "grp", None, None, None),
        P("strat", "grp", None),
        P("strat", "grp", None, None, None, None),
    )
    return jax.shard_map(
        per_device,
        mesh=mesh,
        in_specs=placed,
        out_specs=(P(("strat", "grp"), None), P("strat", None)),
        check_vma=False,
    )
```

profile of v0, /device:TPU:1, one launch (start us, length us, event | category | flops | bytes accessed | tf_op | source)
XLA Modules:
  0.0 752.5 jit_solution(12786251001411020271)
XLA Ops:
  7.2 0.0 all-reduce.4.cloned.1.call-start
  7.2 0.8 slice_bitcast_fusion
  8.0 0.8 compare_and_fusion
  8.8 1.4 fusion.68
  10.1 0.6 iota_compare_fusion.8
  10.8 1.3 convert_element_type.53
  12.1 2.4 convert_element_type.54
  14.5 1.6 gather_fusion
  16.1 0.6 gather_fusion.1
  16.7 0.0 copy-start.3
  16.7 2.0 fusion.12
  18.7 0.0 copy-done.3
  18.7 0.5 fusion.21
  19.2 2.9 fusion.8
  22.1 4.4 copy.8
  26.6 0.0 all-reduce.4.cloned.1.call-update
  26.6 0.0 all-reduce.6.cloned.1.call-start
  26.6 190.7 %all-reduce.4.cloned.1.call-done = f32[4096,256]{1,0:T(8,128)} async-done(((f32[4096,256]{1,0:T(8,128)}), f32[4096,256]{1,0:T(8,128)}) %all-reduce.4.cloned.1.call-update) | async-done | bytes 4194320 | tf_op jit(solution)/shard_map/psum | solution.py:53
  217.3 6.2 multiply_subtract_fusion.2
  223.5 0.8 collective-permute-start
  224.3 0.5 fusion.22
  224.8 0.0 copy-start
  224.8 2.0 fusion.10
  226.8 0.3 copy.7
  227.2 0.2 fusion.27
  227.3 1.6 gather_fusion.2
  228.9 0.6 iota_compare_fusion.7
  229.5 43.7 %collective-permute-done = f32[4096,256]{1,0:T(8,128)} collective-permute-done((f32[4096,256]{1,0:T(8,128)}, f32[4096,256]{1,0:T(8,128)}, u32[]{:S(2)}, u32[]{:S(2)}) %collective-permute-start) | collective-permute-done | bytes 4194336 | tf_op jit(solution)/shard_map/ppermute | solution.py:10
  273.2 3.7 convert_element_type.59
  276.9 2.2 gather_fusion.3
  279.1 0.0 copy-start.1
  279.1 2.0 fusion.13
  281.1 0.0 copy-start.4
  281.1 0.5 fusion.23
  281.6 0.3 copy-done.4
  281.9 2.9 fusion.4
  284.9 4.4 copy.10
  289.3 0.0 all-reduce.6.cloned.1.call-update
  289.3 0.0 all-reduce.8.cloned.1.call-start
  289.4 188.5 %all-reduce.6.cloned.1.call-done = f32[4096,256]{1,0:T(8,128)} async-done(((f32[4096,256]{1,0:T(8,128)}), f32[4096,256]{1,0:T(8,128)}) %all-reduce.6.cloned.1.call-update) | async-done | bytes 4194320 | tf_op jit(solution)/shard_map/psum | solution.py:53
  477.9 6.2 multiply_subtract_fusion.1
  484.1 0.8 collective-permute-start.1
  484.9 0.6 iota_compare_fusion.6
  485.5 0.5 fusion.24
  486.1 2.0 fusion.6
  488.0 0.3 copy.9
  488.4 1.1 fusion.67
  489.5 2.6 gather_fusion.4
  492.1 41.7 %collective-permute-done.1 = f32[4096,256]{1,0:T(8,128)} collective-permute-done((f32[4096,256]{1,0:T(8,128)}, f32[4096,256]{1,0:T(8,128)}, u32[]{:S(2)}, u32[]{:S(2)}) %collective-permute-start.1) | collective-permute-done | bytes 4194336 | tf_op jit(solution)/shard_map/ppermute | solution.py:10
  533.8 3.7 convert_element_type.64
  537.5 3.3 gather_fusion.5
  540.8 2.3 fusion.14
  543.1 0.0 copy-start.6
  543.1 0.5 fusion.25
  543.6 0.3 copy-done.6
  543.9 2.9 fusion
  546.8 4.4 copy.12
  551.3 0.0 all-reduce.8.cloned.1.call-update
  551.3 1.9 fusion.26
  553.2 2.0 fusion.2
  555.2 0.3 copy.11
  555.5 1.4 fusion.16
  556.9 182.9 %all-reduce.8.cloned.1.call-done = f32[4096,256]{1,0:T(8,128)} async-done(((f32[4096,256]{1,0:T(8,128)}), f32[4096,256]{1,0:T(8,128)}) %all-reduce.8.cloned.1.call-update) | async-done | bytes 4194320 | tf_op jit(solution)/shard_map/psum | solution.py:53
  739.8 6.2 multiply_subtract_fusion
  (9 shorter events, 0.0 us)
Async XLA Ops:
  7.2 210.1 %all-reduce.4.cloned.1.call-start = ((), (), s32[]{:S(2)}) async-start(), calls=%async_computation | async-start | bytes 8388608 | tf_op jit(solution)/shard_map/psum | solution.py:53
  16.7 2.0 copy-start.3
  26.6 451.3 %all-reduce.6.cloned.1.call-start = ((), (), s32[]{:S(2)}) async-start(), calls=%async_computation.1 | async-start | bytes 8388608 | tf_op jit(solution)/shard_map/psum | solution.py:53
  223.5 49.8 %collective-permute-start = (f32[4096,256]{1,0:T(8,128)}, f32[4096,256]{1,0:T(8,128)}, u32[]{:S(2)}, u32[]{:S(2)}) collective-permute-start(f32[4096,256]{1,0:T(8,128)} %multiply_subtract_fusion.2), channel_id=1, source_target_pairs={{8,0},{16,8},{24,16},{32,24},{40,32},{48,40},{56,48},{64,56},{72,6... | collective-permute-start | bytes 12582920 | tf_op jit(solution)/shard_map/ppermute | solution.py:10
  224.8 2.4 copy-start
  279.1 2.0 copy-start.1
  281.1 0.8 copy-start.4
  289.3 450.5 %all-reduce.8.cloned.1.call-start = ((), (), s32[]{:S(2)}) async-start(), calls=%async_computation.2 | async-start | bytes 8388608 | tf_op jit(solution)/shard_map/psum | solution.py:53
  477.9 7.7 %copy-start.5 = (bf16[16,128,128]{2,1,0:T(8,128)(2,1)S(1)}, bf16[16,128,128]{2,1,0:T(8,128)(2,1)}, u32[]{:S(2)}) copy-start(bf16[16,128,128]{2,1,0:T(8,128)(2,1)} %copy-done.4) | copy-start | bytes 1572868
  484.1 49.8 %collective-permute-start.1 = (f32[4096,256]{1,0:T(8,128)}, f32[4096,256]{1,0:T(8,128)}, u32[]{:S(2)}, u32[]{:S(2)}) collective-permute-start(f32[4096,256]{1,0:T(8,128)} %multiply_subtract_fusion.1), channel_id=1, source_target_pairs={{8,0},{16,8},{24,16},{32,24},{40,32},{48,40},{56,48},{64,56},{72,6... | collective-permute-start | bytes 12582920 | tf_op jit(solution)/shard_map/ppermute | solution.py:10
  540.8 2.3 copy-start.2
  543.1 0.8 copy-start.6
Sparse Core Ops, SparseCore 0:
  26.7 190.5 all-reduce.3
  289.4 188.3 all-reduce.5
  551.4 188.3 all-reduce.7
where the time goes:
time: 753 us
  waiting for transfers between devices  648 us (86%)
  other arithmetic  34.9 us (5%)
  local copies, waits for them, and re-layouts  28.9 us (4%)
  matrix products  25.3 us (3%)
  between operations  14 us (2%)
    psum x3, waiting for transfers between devices, per_device(): total = lax.psum(item_grad, 'grp')  562 us
    ppermute x2, waiting for transfers between devices, from_behind(): return lax.ppermute(block, axis, route)  85.4 us
    sub x3, other arithmetic, per_device(): slab = slab - 0.003 * (0.05 * slab - total)  18.5 us
  transfers between devices with their start and end apart: 5, of which 5 were waited for; matrix products, arithmetic and copies ran while one was open for 2% of the time, Pallas kernels for 0%

commit v1 on v0

v1 whole, which is shorter than its diff:
```python
import jax
import jax.numpy as jnp
from jax import lax
from jax.experimental import pallas as pl
from jax.experimental.pallas import tpu as pltpu
from jax.sharding import PartitionSpec as P

MESH = pl.DeviceIdType.MESH
F32 = jnp.float32
BF16 = jnp.bfloat16
RATE = 0.003
DECAY = 0.05
SEMS = 256


def step_of(value, grad):
    return value - RATE * (DECAY * value - grad)


def kernel(
    strata, tab_s, tab_v, users, slab, vals, users_out, items_out,
    uf, uc, uo, ug, ub, vb, res, res_t, lhs, grad, vals_out, vals_in, tab_in, tab_c,
    rb0, rb1, rb2, sib1, sib2, part, vu0, vu1, vu2, vn1, vn2, out, ssem, rsem, lsem,
):
    s, g = lax.axis_index("strat"), lax.axis_index("grp")
    core, yhi, x, ylo = s % 2, (s // 2) % 2, g // 2, g % 2
    base = s - core
    side = (ylo + yhi) % 2
    keeps = core == side
    moves = core != side
    rx, lx, ox = (x + 1) % 4, (x + 3) % 4, (x + 2) % 4
    right, left = (s, rx * 2 + ylo), (s, lx * 2 + ylo)
    sibling = (base + 1 - core, g)
    across = (s, x * 2 + 1 - ylo)
    swap = (base + 1 - core, x * 2 + 1 - ylo)
    ahead = (s + strata - 2) % strata
    behind = (s + 2) % strata

    barrier = pltpu.get_barrier_semaphore()

    def greet(device):
        pl.semaphore_signal(barrier, inc=1, device_id=device, device_id_type=MESH)

    for device in (right, left, sibling, across, swap):
        greet(device)

    @pl.when(side == 0)
    def _():
        greet((ahead, g))

    @pl.when(side == 1)
    def _():
        greet((behind, g))
        greet(((base + 2) % strata, x * 2 + 1 - ylo))

    @pl.when((side == 1) & (core == 0))
    def _():
        greet((ahead, x * 2 + 1 - ylo))
        greet((ahead + 1, x * 2 + 1 - ylo))

    pl.semaphore_wait(barrier, 6 + side * (1 + 2 * (1 - core)))

    def rc(src, dst, si, ri, device):
        return pltpu.make_async_remote_copy(
            src_ref=src, dst_ref=dst, send_sem=ssem.at[si], recv_sem=rsem.at[ri],
            device_id=device, device_id_type=MESH,
        )

    def arrived(ref, ri):
        rc(ref, ref, 0, ri, right).wait_recv()

    counts = {"s": 0, "r": 0}

    def take(kind, n):
        counts[kind] += n
        assert counts[kind] <= SEMS
        return counts[kind] - n

    def each(n, body):
        @pl.loop(0, n)
        def _(i):
            body(i)

    def residuals(tab, values):
        def one(n):
            u = ub[tab(0, 32 + n)]
            v = vb[tab(0, 48 + n)]
            guess = lax.dot_general(u, v, (((1,), (1,)), ((), ())), preferred_element_type=F32)
            left_over = values(n).astype(F32) - guess
            res[n] = left_over.astype(BF16)
            res_t[n] = left_over.T.astype(BF16)

        each(16, one)

    def item_quad(tab, q):
        for i in range(4):
            for a in range(8):
                lhs[i * 128:(i + 1) * 128, a * 128:(a + 1) * 128] = res_t[tab(a, q * 4 + i)]
        total = jnp.dot(lhs[...], ub[...].reshape(1024, 256), preferred_element_type=F32)
        grad[pl.ds(q * 4, 4)] = total.reshape(4, 128, 256)

    def user_grads(tab):
        def one(w):
            half, c = w // 4, w % 4
            for i in range(4):
                for j in range(8):
                    lhs[i * 128:(i + 1) * 128, j * 128:(j + 1) * 128] = res[tab(half * 4 + i, c * 8 + j)]
            block = vb[pl.ds(c * 8, 8)].reshape(1024, 256)
            total = jnp.dot(lhs[...], block, preferred_element_type=F32)
            spot = pl.ds(half * 4, 4)
            ug[spot] = ug[spot] + total.reshape(4, 128, 256)

        ug[...] = jnp.zeros_like(ug)
        each(8, one)

    class Ring:
        def __init__(self, tile, m, rb):
            self.tile, self.m, self.rb = tile, m, rb
            self.so, self.ro = take("s", 6 * m), take("r", 6 * m)

        def go(self, chunk, j, slot, k, device):
            return rc(grad.at[self.tile(chunk, j)], self.rb.at[slot], self.so + k, self.ro + slot, device)

        def opp_r(self, j):
            return self.go(ox, j, j, j, right)

        def opp_l(self, j):
            return self.go(ox, self.m + j, self.m + j, self.m + j, left)

        def mid_r(self, j):
            return self.go(rx, self.m + j, 3 * self.m + j, 2 * self.m + j, right)

        def mid_l(self, j):
            return self.go(lx, j, 4 * self.m + j, 3 * self.m + j, left)

        def end_r(self, j):
            return self.go(rx, j, 2 * self.m + j, 4 * self.m + j, right)

        def end_l(self, j):
            return self.go(lx, self.m + j, 5 * self.m + j, 5 * self.m + j, left)

        def landed(self, slot):
            arrived(self.rb.at[slot], self.ro + slot)

        def start_opp(self):
            each(self.m, lambda j: (self.opp_r(j).start(), self.opp_l(j).start()))

        def start_mid_r(self):
            each(self.m, lambda j: self.mid_r(j).start())

        def start_mid_l(self):
            each(self.m, lambda j: self.mid_l(j).start())

        def relay(self):
            def one(j):
                self.landed(j)
                spot = self.tile(rx, j)
                grad[spot] = grad[spot] + self.rb[j]
                self.end_r(j).start()
                self.landed(self.m + j)
                spot = self.tile(lx, self.m + j)
                grad[spot] = grad[spot] + self.rb[self.m + j]
                self.end_l(j).start()

            each(self.m, one)

        def finish(self, done):
            m = self.m

            def one(j):
                self.landed(4 * m + j)
                self.landed(2 * m + j)
                done(j, grad[self.tile(x, j)] + self.rb[2 * m + j] + self.rb[4 * m + j])
                self.landed(3 * m + j)
                self.landed(5 * m + j)
                done(m + j, grad[self.tile(x, m + j)] + self.rb[3 * m + j] + self.rb[5 * m + j])

            each(m, one)

        def drain(self):
            def one(j):
                for f in (self.opp_r, self.opp_l, self.mid_r, self.mid_l, self.end_r, self.end_l):
                    f(j).wait_send()

            each(self.m, one)

    class Spread:
        def __init__(self, buf, half, extra):
            self.buf, self.half, self.extra = buf, half, extra
            self.so, self.ro = take("s", 12), take("r", 12)

        def at(self, chunk, p):
            return self.buf.at[chunk * 8 + self.half * 4 + p]

        def own_r(self, p):
            return rc(self.at(x, p), self.at(x, p), self.so + p, self.ro + p, right)

        def own_l(self, p):
            return rc(self.at(x, p), self.at(x, p), self.so + 4 + p, self.ro + 4 + p, left)

        def fwd_r(self, p):
            return rc(self.at(lx, p), self.at(lx, p), self.so + 8 + p, self.ro + 8 + p, right)

        def fwd_l(self, p):
            return rc(self.at(rx, 2 + p), self.at(rx, 2 + p), self.so + 10 + p, self.ro + 10 + p, left)

        def own(self, p):
            self.own_r(p).start()
            self.own_l(p).start()

        def rest(self):
            def first(p):
                arrived(self.at(lx, p), self.ro + p)
                self.fwd_r(p).start()
                self.extra(lx, p)
                arrived(self.at(rx, 2 + p), self.ro + 6 + p)
                self.fwd_l(p).start()
                self.extra(rx, 2 + p)

            def second(p):
                arrived(self.at(lx, 2 + p), self.ro + 2 + p)
                self.extra(lx, 2 + p)
                arrived(self.at(rx, p), self.ro + 4 + p)
                self.extra(rx, p)

            def third(p):
                arrived(self.at(ox, p), self.ro + 8 + p)
                self.extra(ox, p)
                arrived(self.at(ox, 2 + p), self.ro + 10 + p)
                self.extra(ox, 2 + p)

            each(2, first)
            each(2, second)
            each(2, third)

        def drain(self):
            def one(p):
                self.own_r(p).wait_send()
                self.own_l(p).wait_send()

            each(4, one)

            def two(p):
                self.fwd_r(p).wait_send()
                self.fwd_l(p).wait_send()

            each(2, two)

    def first_tab(a, t):
        return tab_s[0, a, t]

    ub[...] = users[...].astype(BF16)

    def cast_slab(t):
        vb[t] = slab[t].astype(BF16)

    each(32, cast_slab)
    res[16] = jnp.zeros((128, 128), BF16)
    res_t[16] = jnp.zeros((128, 128), BF16)
    residuals(first_tab, lambda n: vals[0, n])

    ring = Ring(lambda c, j: c * 8 + j, 4, rb0)

    def chunk_grads(tab, c):
        each(2, lambda h: item_quad(tab, c * 2 + h))

    chunk_grads(first_tab, ox)
    ring.start_opp()
    chunk_grads(first_tab, rx)
    ring.start_mid_r()
    chunk_grads(first_tab, lx)
    ring.start_mid_l()
    chunk_grads(first_tab, x)

    move_s, move_r = take("s", 4), take("r", 4)
    move_tab = rc(tab_v, tab_in, move_s, move_r, swap)
    move_val = [rc(vals_out.at[i], vals_in.at[i], move_s + 1 + i, move_r + 1 + i, swap) for i in range(2)]
    move_users = rc(uf, uc, move_s + 3, move_r + 3, swap)

    @pl.when(moves)
    def _():
        move_tab.start()

        def one(n):
            vals_out[0, n] = vals[1, n].astype(F32)
            vals_out[1, n] = vals[2, n].astype(F32)

        each(16, one)
        move_val[0].start()

    @pl.when(keeps)
    def _():
        def one(n):
            vals_in[0, n] = vals[1, n].astype(F32)
            vals_in[1, n] = vals[2, n].astype(F32)

        each(16, one)
        tab_in[...] = tab_v[...]

    user_grads(first_tab)

    @pl.when(moves)
    def _():
        each(8, lambda a: uf.__setitem__(a, step_of(users[a], ug[a])))
        move_users.start()
        move_val[1].start()

    @pl.when(keeps)
    def _():
        each(8, lambda a: uc.__setitem__(a, step_of(users[a], ug[a])))

    ring.relay()

    part_s, part_r = take("s", 8), take("r", 8)
    shift_s, shift_r = take("s", 8), take("r", 4)

    def part_copy(j):
        return rc(vu0.at[j], part.at[j], part_s + j, part_r + j, across)

    def shift0(j):
        h, p = j // 4, j % 4
        target = ((base + strata - 2 * side + h) % strata, x * 2 + yhi)
        return rc(vu0.at[j], vn1.at[x * 8 + j], shift_s + j, shift_r + p, target)

    def shift_self(j):
        return pltpu.make_async_copy(vu0.at[j], vn1.at[x * 8 + j], rsem.at[shift_r + j % 4])

    def to_self(j):
        return (side == 0) & (j // 4 == 1)

    def summed(j, total):
        @pl.when(keeps)
        def _():
            vu0[j] = total
            part_copy(j).start()

        @pl.when(moves)
        def _():
            arrived(part.at[j], part_r + j)
            vu0[j] = step_of(slab[x * 8 + j], total + part[j])

            @pl.when(to_self(j))
            def _():
                shift_self(j).start()

            @pl.when(jnp.logical_not(to_self(j)))
            def _():
                shift0(j).start()

    ring.finish(summed)
    ring.drain()

    def gather(vn, arrive_r):
        sib_s, sib_r = take("s", 16), take("r", 16)

        def to_sib(chunk, p):
            spot = vn.at[chunk * 8 + core * 4 + p]
            return rc(spot, spot, sib_s + chunk * 4 + p, sib_r + chunk * 4 + p, sibling)

        def take_in(chunk, p):
            to_sib(chunk, p).start()
            t = chunk * 8 + core * 4 + p
            vb[t] = vn[t].astype(BF16)

        spread = Spread(vn, core, take_in)

        def own(p):
            arrived(vn.at[x * 8 + core * 4 + p], arrive_r + p)
            spread.own(p)
            take_in(x, p)

        each(4, own)
        spread.rest()

        def other(order):
            def one(p):
                t = order * 8 + (1 - core) * 4 + p
                arrived(vn.at[t], sib_r + order * 4 + p)
                vb[t] = vn[t].astype(BF16)

            each(4, one)

        for chunk in (x, lx, rx, ox):
            other(chunk)

        def drain():
            spread.drain()
            each(4, lambda c: each(4, lambda p: to_sib(c, p).wait_send()))

        return drain

    tab_copy = pltpu.make_async_copy(tab_in, tab_c, lsem.at[0])

    def row_step(k, vn, rb, sibs, done):
        def tab(a, t):
            return tab_c[k, a, t]

        for c in range(8):
            ub[c] = uc[c].astype(BF16)
        residuals(tab, lambda n: vals_in[k - 1, n])
        ring = Ring(lambda c, j: c * 8 + core * 4 + j, 2, rb)
        give_s, give_r = take("s", 16), take("r", 16)

        def give(c, p):
            return rc(
                grad.at[c * 8 + (1 - core) * 4 + p], sibs.at[c * 4 + p],
                give_s + c * 4 + p, give_r + c * 4 + p, sibling,
            )

        def compute(c):
            item_quad(tab, c * 2 + 1 - core)
            each(4, lambda p: give(c, p).start())
            item_quad(tab, c * 2 + core)

        def add(c):
            def one(p):
                arrived(sibs.at[c * 4 + p], give_r + c * 4 + p)
                t = c * 8 + core * 4 + p
                grad[t] = grad[t] + sibs[c * 4 + p]

            each(4, one)

        compute(ox)
        compute(rx)
        add(ox)
        ring.start_opp()
        compute(lx)
        add(rx)
        ring.start_mid_r()
        compute(x)
        add(lx)
        ring.start_mid_l()
        user_grads(tab)

        def update(a):
            uc[a] = step_of(uc[a], ug[a])

        each(8, update)
        if k == 2:
            back = rc(uc, uo, take("s", 1), take("r", 1), swap)

            @pl.when(moves)
            def _():
                back.start()

            @pl.when(keeps)
            def _():
                uo[...] = uc[...]

        ring.relay()
        add(x)

        def finish(p, total):
            done(p, step_of(vn[x * 8 + core * 4 + p], total))

        ring.finish(finish)
        ring.drain()
        each(4, lambda c: each(4, lambda p: give(c, p).wait_send()))
        if k == 2:
            return back

    drain1 = gather(vn1, shift_r)

    @pl.when(moves)
    def _():
        move_tab.wait_recv()
        move_val[0].wait_recv()
        move_users.wait_recv()
        move_tab.wait_send()
        move_val[0].wait_send()
        move_users.wait_send()

    tab_copy.start()
    tab_copy.wait()

    next_s, next_r = take("s", 4), take("r", 4)

    def shift1(p):
        target = ((s + strata - 2 * (1 - side)) % strata, x * 2 + yhi)
        return rc(vu1.at[p], vn2.at[x * 8 + core * 4 + p], next_s + p, next_r + p, target)

    def done1(p, value):
        vu1[p] = value
        shift1(p).start()

    row_step(1, vn1, rb1, sib1, done1)
    drain2 = gather(vn2, next_r)

    @pl.when(moves)
    def _():
        move_val[1].wait_recv()
        move_val[1].wait_send()

    last_s, last_r = take("s", 4), take("r", 4)
    cross_s, cross_r = take("s", 20), take("r", 20)

    def home(p):
        return rc(vu2.at[p], out.at[x * 8 + core * 4 + p], last_s + p, last_r + p, sibling)

    def cross_a(p):
        spot = out.at[x * 8 + core * 4 + p]
        return rc(spot, spot, cross_s + p, cross_r + p, across)

    def cross_b(c, p):
        spot = out.at[c * 8 + (1 - core) * 4 + p]
        k = 4 + c * 4 + p
        return rc(spot, spot, cross_s + k, cross_r + k, across)

    def emit(t):
        return pltpu.make_async_copy(out.at[t], items_out.at[t], lsem.at[1 + t])

    near = Spread(out, core, lambda c, p: emit(c * 8 + core * 4 + p).start())

    def far_extra(c, p):
        cross_b(c, p).start()
        emit(c * 8 + (1 - core) * 4 + p).start()

    far = Spread(out, 1 - core, far_extra)

    def done2(p, value):
        @pl.when(keeps)
        def _():
            out[x * 8 + core * 4 + p] = value
            near.own(p)
            cross_a(p).start()
            emit(x * 8 + core * 4 + p).start()

        @pl.when(moves)
        def _():
            vu2[p] = value
            home(p).start()

    back = row_step(2, vn2, rb2, sib2, done2)

    @pl.when(keeps)
    def _():
        def one(p):
            arrived(out.at[x * 8 + (1 - core) * 4 + p], last_r + p)
            far.own(p)
            far_extra(x, p)

        each(4, one)

    @pl.when(moves)
    def _():
        each(4, lambda p: home(p).wait_send())

        def one(p):
            t = x * 8 + core * 4 + p
            arrived(out.at[t], cross_r + p)
            near.own(p)
            emit(t).start()

        each(4, one)

    near.rest()

    @pl.when(keeps)
    def _():
        far.rest()

    @pl.when(moves)
    def _():
        def some(c):
            def one(p):
                t = c * 8 + (1 - core) * 4 + p
                arrived(out.at[t], cross_r + 4 + c * 4 + p)
                emit(t).start()

            each(4, one)

        for c in (x, lx, rx, ox):
            some(c)
        back.wait_recv()
        back.wait_send()

    users_copy = pltpu.make_async_copy(uo, users_out, lsem.at[0])
    users_copy.start()

    drain1()
    drain2()
    near.drain()
    each(4, lambda p: shift1(p).wait_send())

    @pl.when(keeps)
    def _():
        each(8, lambda j: part_copy(j).wait_send())
        far.drain()
        each(4, lambda p: cross_a(p).wait_send())
        each(4, lambda c: each(4, lambda p: cross_b(c, p).wait_send()))

    @pl.when(moves)
    def _():
        def one(j):
            @pl.when(jnp.logical_not(to_self(j)))
            def _():
                shift0(j).wait_send()

        each(8, one)

    each(32, lambda t: emit(t).wait())
    users_copy.wait()


def tables(coords, counts):
    order = jnp.arange(16, dtype=jnp.int32)
    live = order[None, :] < counts[:, None]
    a = jnp.clip(coords[:, 0], 0, 7)
    b = jnp.clip(coords[:, 1], 0, 31)
    hit = (
        (a[:, None, None, :] == jnp.arange(8, dtype=jnp.int32)[None, :, None, None])
        & (b[:, None, None, :] == jnp.arange(32, dtype=jnp.int32)[None, None, :, None])
        & live[:, None, None, :]
    )
    spot = jnp.min(jnp.where(hit, order, 16), axis=-1)
    wide = lambda v: jnp.broadcast_to(v[:, None, :], (3, 8, 16))
    return jnp.concatenate([spot, wide(a), wide(b), jnp.zeros((3, 8, 64), jnp.int32)], axis=-1)


def per_device(strata, user_factors, item_factors, tile_coords, tile_counts, tile_values):
    tab = tables(tile_coords[0, 0], tile_counts[0, 0])
    vmem = pl.BlockSpec(memory_space=pltpu.VMEM)
    smem = pl.BlockSpec(memory_space=pltpu.SMEM)
    anywhere = pl.BlockSpec(memory_space=pl.ANY)
    tiles = lambda n: pltpu.VMEM((n, 128, 256), F32)
    users, items = pl.pallas_call(
        lambda *refs: kernel(strata, *refs),
        out_shape=(
            jax.ShapeDtypeStruct((8, 128, 256), F32),
            jax.ShapeDtypeStruct((32, 128, 256), F32),
        ),
        in_specs=[smem, vmem, vmem, vmem, vmem],
        out_specs=(anywhere, anywhere),
        scratch_shapes=[
            tiles(8), tiles(8), tiles(8), tiles(8),
            pltpu.VMEM((8, 128, 256), BF16),
            pltpu.VMEM((32, 128, 256), BF16),
            pltpu.VMEM((17, 128, 128), BF16),
            pltpu.VMEM((17, 128, 128), BF16),
            pltpu.VMEM((512, 1024), BF16),
            tiles(32),
            pltpu.VMEM((2, 16, 128, 128), F32),
            pltpu.VMEM((2, 16, 128, 128), F32),
            pltpu.VMEM((3, 8, 128), jnp.int32),
            pltpu.SMEM((3, 8, 128), jnp.int32),
            tiles(24), tiles(12), tiles(12), tiles(16), tiles(16),
            tiles(8), tiles(8), tiles(4), tiles(4),
            tiles(32), tiles(32), tiles(32),
            pltpu.SemaphoreType.DMA((SEMS,)),
            pltpu.SemaphoreType.DMA((SEMS,)),
            pltpu.SemaphoreType.DMA((33,)),
        ],
        compiler_params=pltpu.CompilerParams(
            collective_id=0, has_side_effects=True, vmem_limit_bytes=67043328
        ),
    )(
        tab, tab,
        user_factors.reshape(8, 128, 256),
        item_factors.reshape(32, 128, 256),
        tile_values[0, 0],
    )
    return users.reshape(1024, 256), items.reshape(4096, 256)


def solution(mesh):
    strata = mesh.shape["strat"]
    placed = (
        P(("strat", "grp"), None),
        P("strat", None),
        P("strat", "grp", None, None, None),
        P("strat", "grp", None),
        P("strat", "grp", None, None, None, None),
    )
    return jax.shard_map(
        lambda *args: per_device(strata, *args),
        mesh=mesh,
        in_specs=placed,
        out_specs=(P(("strat", "grp"), None), P("strat", None)),
        check_vma=False,
    )
```

time: 753 us -> 218 us (0.29)
  the two profiles are of different devices: /device:TPU:1 before, /device:TPU:8 now
where the time goes in v1:
time: 218 us
  Pallas kernels  208 us (95%)
  local copies, waits for them, and re-layouts  6.82 us (3%)
  other arithmetic  2.44 us (1%)
    pallas_call x1, Pallas kernels, per_device(): pl.pallas_call(lambda *refs: kernel(strata, *refs), out_shape=(jax.ShapeD...  208 us
    unnamed x3, local copies, waits for them, and re-layouts  6.74 us

profile of v1, /device:TPU:8, one launch (start us, length us, event | category | flops | bytes accessed | tf_op | source)
XLA Modules:
  0.0 218.0 jit_solution(2470356220189044551)
XLA Ops:
  0.6 0.7 iota_compare_fusion.2
  1.4 0.1 pad.3.clone
  1.4 0.8 slice_clamp_fusion.1
  2.2 0.1 iota_compare_fusion
  2.3 0.2 select_reduce_fusion
  2.5 0.7 add_add_fusion.refs_0_.refs_1_
  3.2 208.0 %shard_map.68 = (f32[8,128,256]{2,1,0:T(8,128)}, f32[32,128,256]{2,1,0:T(8,128)}) custom-call(s32[3,8,128]{2,1,0:T(8,128)} %add_add_fusion.refs_0_.refs_1_, s32[3,8,128]{2,1,0:T(8,128)} %add_add_fusion.refs_0_.refs_1_, f32[8,128,256]{2,1,0:T(8,128)} %bitcast.15, f32[32,128,256]{2,1,0:T(8,128)} %bitcast.11, bf16[3,16,128,128]{3,2,1,0:T(8,128)(2,1)} %bitcast.13), custom_call_target="tpu_custom_call" | custom-call | tf_op jit(solution)/shard_map/pallas_call | solution.py:626
  211.2 2.3 %copy.13 = f32[1024,256]{1,0:T(8,128)} copy(f32[1024,256]{1,0:T(8,128)} %bitcast.14) | data formatting | bytes 2097152
  213.5 4.5 %copy.14 = f32[4096,256]{1,0:T(8,128)} copy(f32[4096,256]{1,0:T(8,128)} %bitcast.12) | data formatting | bytes 8388608
  (5 shorter events, 0.0 us)

commit v2 on v1

--- a/solution.py
+++ b/solution.py
@@ -11,6 +11,7 @@
 RATE = 0.003
 DECAY = 0.05
 SEMS = 256
+VMEM_BYTES = 54 * 2**20
 
 
 def step_of(value, grad):
@@ -18,9 +19,9 @@
 
 
 def kernel(
-    strata, tab_s, tab_v, users, slab, vals, users_out, items_out,
-    uf, uc, uo, ug, ub, vb, res, res_t, lhs, grad, vals_out, vals_in, tab_in, tab_c,
-    rb0, rb1, rb2, sib1, sib2, part, vu0, vu1, vu2, vn1, vn2, out, ssem, rsem, lsem,
+    strata, coords, counts, users_in, slab_in, vals_in_hbm, uo, out,
+    users, slab, vals, tab_v, uf, uc, ug, ub, vb, res, res_t, lhs, grad, vals_out, vals_in, tab_in, tab_c,
+    rb0, rb1, rb2, sib1, sib2, part, vu0, vu1, vu2, rel, vn1, vn2, ssem, rsem, lsem,
 ):
     s, g = lax.axis_index("strat"), lax.axis_index("grp")
     core, yhi, x, ylo = s % 2, (s // 2) % 2, g // 2, g % 2
@@ -36,6 +37,15 @@
     ahead = (s + strata - 2) % strata
     behind = (s + 2) % strata
 
+    def fetch(src, dst, k):
+        copy = pltpu.make_async_copy(src, dst, lsem.at[k])
+        copy.start()
+        return copy
+
+    get_vals = [fetch(vals_in_hbm.at[k], vals.at[k], k) for k in (1, 0, 2)]
+    get_users = fetch(users_in, users, 3)
+    get_slab = fetch(slab_in, slab, 4)
+
     barrier = pltpu.get_barrier_semaphore()
 
     def greet(device):
@@ -44,21 +54,33 @@
     for device in (right, left, sibling, across, swap):
         greet(device)
 
-    @pl.when(side == 0)
-    def _():
-        greet((ahead, g))
-
     @pl.when(side == 1)
     def _():
-        greet((behind, g))
-        greet(((base + 2) % strata, x * 2 + 1 - ylo))
-
-    @pl.when((side == 1) & (core == 0))
-    def _():
         greet((ahead, x * 2 + 1 - ylo))
-        greet((ahead + 1, x * 2 + 1 - ylo))
-
-    pl.semaphore_wait(barrier, 6 + side * (1 + 2 * (1 - core)))
+        greet((behind, x * 2 + 1 - ylo))
+        greet(((s + strata - 1 + 2 * core) % strata, x * 2 + 1 - ylo))
+
+    rows = lax.broadcasted_iota(jnp.int32, (8, 128), 0)
+    cols = lax.broadcasted_iota(jnp.int32, (8, 128), 1)
+
+    def user_tile(k, n):
+        return jnp.clip(coords[k, 0, n], 0, 7)
+
+    def item_tile(k, n):
+        return jnp.clip(coords[k, 1, n], 0, 31)
+
+    for k in range(3):
+        table = jnp.full((8, 128), 16, jnp.int32)
+        for n in range(16):
+            a, b = user_tile(k, n), item_tile(k, n)
+            spot = jnp.where(n < counts[k], b, 1000)
+            table = jnp.where((rows == a) & (cols == spot), n, table)
+            table = jnp.where(cols == 32 + n, a, table)
+            table = jnp.where(cols == 48 + n, b, table)
+        tab_v[k] = table
+    tab_copy0 = fetch(tab_v.at[0], tab_c.at[0], 5)
+
+    pl.semaphore_wait(barrier, 5 + 3 * side)
 
     def rc(src, dst, si, ri, device):
         return pltpu.make_async_remote_copy(
@@ -69,28 +91,28 @@
     def arrived(ref, ri):
         rc(ref, ref, 0, ri, right).wait_recv()
 
-    counts = {"s": 0, "r": 0}
+    taken = {"s": 0, "r": 0}
 
     def take(kind, n):
-        counts[kind] += n
-        assert counts[kind] <= SEMS
-        return counts[kind] - n
+        taken[kind] += n
+        assert taken[kind] <= SEMS
+        return taken[kind] - n
 
     def each(n, body):
         @pl.loop(0, n)
         def _(i):
             body(i)
 
-    def residuals(tab, values):
+    def residuals(user_at, item_at, values):
         def one(n):
-            u = ub[tab(0, 32 + n)]
-            v = vb[tab(0, 48 + n)]
+            u = ub[user_at(n)]
+            v = vb[item_at(n)]
             guess = lax.dot_general(u, v, (((1,), (1,)), ((), ())), preferred_element_type=F32)
             left_over = values(n).astype(F32) - guess
             res[n] = left_over.astype(BF16)
             res_t[n] = left_over.T.astype(BF16)
 
-        each(16, one)
+        each(4, lambda i: [one(i * 4 + j) for j in range(4)])
 
     def item_quad(tab, q):
         for i in range(4):
@@ -247,17 +269,37 @@
             each(2, two)
 
     def first_tab(a, t):
-        return tab_s[0, a, t]
-
+        return tab_c[0, a, t]
+
+    move_s, move_r = take("s", 4), take("r", 4)
+    move_tab = rc(tab_v, tab_in, move_s, move_r, swap)
+    move_val = [rc(vals_out.at[i], vals_in.at[i], move_s + 1 + i, move_r + 1 + i, swap) for i in range(2)]
+    move_users = rc(uf, uc, move_s + 3, move_r + 3, swap)
+
+    def widen(dst, k):
+        each(4, lambda i: dst.__setitem__((k - 1, pl.ds(i * 4, 4)), vals[k, pl.ds(i * 4, 4)].astype(F32)))
+
+    get_vals[0].wait()
+
+    @pl.when(moves)
+    def _():
+        widen(vals_out, 1)
+        move_val[0].start()
+        move_tab.start()
+
+    get_users.wait()
     ub[...] = users[...].astype(BF16)
+    get_slab.wait()
 
     def cast_slab(t):
         vb[t] = slab[t].astype(BF16)
 
     each(32, cast_slab)
+    get_vals[1].wait()
+    residuals(lambda n: user_tile(0, n), lambda n: item_tile(0, n), lambda n: vals[0, n])
     res[16] = jnp.zeros((128, 128), BF16)
     res_t[16] = jnp.zeros((128, 128), BF16)
-    residuals(first_tab, lambda n: vals[0, n])
+    tab_copy0.wait()
 
     ring = Ring(lambda c, j: c * 8 + j, 4, rb0)
 
@@ -272,43 +314,19 @@
     ring.start_mid_l()
     chunk_grads(first_tab, x)
 
-    move_s, move_r = take("s", 4), take("r", 4)
-    move_tab = rc(tab_v, tab_in, move_s, move_r, swap)
-    move_val = [rc(vals_out.at[i], vals_in.at[i], move_s + 1 + i, move_r + 1 + i, swap) for i in range(2)]
-    move_users = rc(uf, uc, move_s + 3, move_r + 3, swap)
-
-    @pl.when(moves)
-    def _():
-        move_tab.start()
-
-        def one(n):
-            vals_out[0, n] = vals[1, n].astype(F32)
-            vals_out[1, n] = vals[2, n].astype(F32)
-
-        each(16, one)
-        move_val[0].start()
-
-    @pl.when(keeps)
-    def _():
-        def one(n):
-            vals_in[0, n] = vals[1, n].astype(F32)
-            vals_in[1, n] = vals[2, n].astype(F32)
-
-        each(16, one)
-        tab_in[...] = tab_v[...]
-
     user_grads(first_tab)
 
     @pl.when(moves)
     def _():
         each(8, lambda a: uf.__setitem__(a, step_of(users[a], ug[a])))
         move_users.start()
-        move_val[1].start()
 
     @pl.when(keeps)
     def _():
         each(8, lambda a: uc.__setitem__(a, step_of(users[a], ug[a])))
-
+        widen(vals_in, 1)
+
+    get_vals[2].wait()
     ring.relay()
 
     part_s, part_r = take("s", 8), take("r", 8)
@@ -348,7 +366,26 @@
                 shift0(j).start()
 
     ring.finish(summed)
+
+    @pl.when(moves)
+    def _():
+        widen(vals_out, 2)
+        move_val[1].start()
+        move_tab.wait_recv()
+        fetch(tab_in.at[pl.ds(1, 2)], tab_c.at[pl.ds(1, 2)], 0)
+        move_users.wait_recv()
+
+    @pl.when(keeps)
+    def _():
+        fetch(tab_v.at[pl.ds(1, 2)], tab_c.at[pl.ds(1, 2)], 0)
+        widen(vals_in, 2)
+
+    def cast_users():
+        each(8, lambda a: ub.__setitem__(a, uc[a].astype(BF16)))
+
+    cast_users()
     ring.drain()
+    pltpu.make_async_copy(tab_v.at[pl.ds(1, 2)], tab_c.at[pl.ds(1, 2)], lsem.at[0]).wait()
 
     def gather(vn, arrive_r):
         sib_s, sib_r = take("s", 16), take("r", 16)
@@ -389,15 +426,11 @@
 
         return drain
 
-    tab_copy = pltpu.make_async_copy(tab_in, tab_c, lsem.at[0])
-
     def row_step(k, vn, rb, sibs, done):
         def tab(a, t):
             return tab_c[k, a, t]
 
-        for c in range(8):
-            ub[c] = uc[c].astype(BF16)
-        residuals(tab, lambda n: vals_in[k - 1, n])
+        residuals(lambda n: tab(0, 32 + n), lambda n: tab(0, 48 + n), lambda n: vals_in[k - 1, n])
         ring = Ring(lambda c, j: c * 8 + core * 4 + j, 2, rb)
         give_s, give_r = take("s", 16), take("r", 16)
 
@@ -407,9 +440,11 @@
                 give_s + c * 4 + p, give_r + c * 4 + p, sibling,
             )
 
-        def compute(c):
+        def theirs(c):
             item_quad(tab, c * 2 + 1 - core)
             each(4, lambda p: give(c, p).start())
+
+        def ours(c):
             item_quad(tab, c * 2 + core)
 
         def add(c):
@@ -420,22 +455,28 @@
 
             each(4, one)
 
-        compute(ox)
-        compute(rx)
+        theirs(ox)
+        ours(ox)
+        theirs(rx)
         add(ox)
         ring.start_opp()
-        compute(lx)
+        ours(rx)
+        theirs(lx)
         add(rx)
         ring.start_mid_r()
-        compute(x)
+        ours(lx)
+        theirs(x)
         add(lx)
         ring.start_mid_l()
+        ours(x)
         user_grads(tab)
 
         def update(a):
             uc[a] = step_of(uc[a], ug[a])
 
         each(8, update)
+        if k == 1:
+            cast_users()
         if k == 2:
             back = rc(uc, uo, take("s", 1), take("r", 1), swap)
 
@@ -463,27 +504,43 @@
 
     @pl.when(moves)
     def _():
-        move_tab.wait_recv()
         move_val[0].wait_recv()
-        move_users.wait_recv()
         move_tab.wait_send()
         move_val[0].wait_send()
         move_users.wait_send()
 
-    tab_copy.start()
-    tab_copy.wait()
-
     next_s, next_r = take("s", 4), take("r", 4)
 
+    rel_s, rel_r = take("s", 4), take("r", 4)
+
     def shift1(p):
-        target = ((s + strata - 2 * (1 - side)) % strata, x * 2 + yhi)
-        return rc(vu1.at[p], vn2.at[x * 8 + core * 4 + p], next_s + p, next_r + p, target)
+        return rc(vu1.at[p], vn2.at[x * 8 + core * 4 + p], next_s + p, next_r + p, across)
+
+    def shift2(p):
+        return rc(vu1.at[p], rel.at[p], next_s + p, rel_r + p, across)
+
+    def shift3(p):
+        target = (ahead, x * 2 + 1 - ylo)
+        return rc(rel.at[p], vn2.at[x * 8 + core * 4 + p], rel_s + p, next_r + p, target)
 
     def done1(p, value):
         vu1[p] = value
-        shift1(p).start()
+
+        @pl.when(side == 1)
+        def _():
+            shift1(p).start()
+
+        @pl.when(side == 0)
+        def _():
+            shift2(p).start()
 
     row_step(1, vn1, rb1, sib1, done1)
+
+    @pl.when(side == 1)
+    def _():
+        for p in (0, 2, 1, 3):
+            arrived(rel.at[p], rel_r + p)
+            shift3(p).start()
     drain2 = gather(vn2, next_r)
 
     @pl.when(moves)
@@ -506,14 +563,10 @@
         k = 4 + c * 4 + p
         return rc(spot, spot, cross_s + k, cross_r + k, across)
 
-    def emit(t):
-        return pltpu.make_async_copy(out.at[t], items_out.at[t], lsem.at[1 + t])
-
-    near = Spread(out, core, lambda c, p: emit(c * 8 + core * 4 + p).start())
+    near = Spread(out, core, lambda c, p: None)
 
     def far_extra(c, p):
         cross_b(c, p).start()
-        emit(c * 8 + (1 - core) * 4 + p).start()
 
     far = Spread(out, 1 - core, far_extra)
 
@@ -523,7 +576,6 @@
             out[x * 8 + core * 4 + p] = value
             near.own(p)
             cross_a(p).start()
-            emit(x * 8 + core * 4 + p).start()
 
         @pl.when(moves)
         def _():
@@ -549,7 +601,6 @@
             t = x * 8 + core * 4 + p
             arrived(out.at[t], cross_r + p)
             near.own(p)
-            emit(t).start()
 
         each(4, one)
 
@@ -565,7 +616,6 @@
             def one(p):
                 t = c * 8 + (1 - core) * 4 + p
                 arrived(out.at[t], cross_r + 4 + c * 4 + p)
-                emit(t).start()
 
             each(4, one)
 
@@ -574,13 +624,14 @@
         back.wait_recv()
         back.wait_send()
 
-    users_copy = pltpu.make_async_copy(uo, users_out, lsem.at[0])
-    users_copy.start()
-
     drain1()
     drain2()
     near.drain()
-    each(4, lambda p: shift1(p).wait_send())
+    each(4, lambda p: shift2(p).wait_send())
+
+    @pl.when(side == 1)
+    def _():
+        each(4, lambda p: shift3(p).wait_send())
 
     @pl.when(keeps)
     def _():
@@ -598,27 +649,8 @@
 
         each(8, one)
 
-    each(32, lambda t: emit(t).wait())
-    users_copy.wait()
-
-
-def tables(coords, counts):
-    order = jnp.arange(16, dtype=jnp.int32)
-    live = order[None, :] < counts[:, None]
-    a = jnp.clip(coords[:, 0], 0, 7)
-    b = jnp.clip(coords[:, 1], 0, 31)
-    hit = (
-        (a[:, None, None, :] == jnp.arange(8, dtype=jnp.int32)[None, :, None, None])
-        & (b[:, None, None, :] == jnp.arange(32, dtype=jnp.int32)[None, None, :, None])
-        & live[:, None, None, :]
-    )
-    spot = jnp.min(jnp.where(hit, order, 16), axis=-1)
-    wide = lambda v: jnp.broadcast_to(v[:, None, :], (3, 8, 16))
-    return jnp.concatenate([spot, wide(a), wide(b), jnp.zeros((3, 8, 64), jnp.int32)], axis=-1)
-
 
 def per_device(strata, user_factors, item_factors, tile_coords, tile_counts, tile_values):
-    tab = tables(tile_coords[0, 0], tile_counts[0, 0])
     vmem = pl.BlockSpec(memory_space=pltpu.VMEM)
     smem = pl.BlockSpec(memory_space=pltpu.SMEM)
     anywhere = pl.BlockSpec(memory_space=pl.ANY)
@@ -626,13 +658,14 @@
     users, items = pl.pallas_call(
         lambda *refs: kernel(strata, *refs),
         out_shape=(
-            jax.ShapeDtypeStruct((8, 128, 256), F32),
-            jax.ShapeDtypeStruct((32, 128, 256), F32),
+            pltpu.VMEM((8, 128, 256), F32),
+            pltpu.VMEM((32, 128, 256), F32),
         ),
-        in_specs=[smem, vmem, vmem, vmem, vmem],
-        out_specs=(anywhere, anywhere),
+        in_specs=[smem, smem, anywhere, anywhere, anywhere],
+        out_specs=(vmem, vmem),
         scratch_shapes=[
-            tiles(8), tiles(8), tiles(8), tiles(8),
+            tiles(8), tiles(32), pltpu.VMEM((3, 16, 128, 128), BF16), pltpu.VMEM((3, 8, 128), jnp.int32),
+            tiles(8), tiles(8), tiles(8),
             pltpu.VMEM((8, 128, 256), BF16),
             pltpu.VMEM((32, 128, 256), BF16),
             pltpu.VMEM((17, 128, 128), BF16),
@@ -644,17 +677,17 @@
             pltpu.VMEM((3, 8, 128), jnp.int32),
             pltpu.SMEM((3, 8, 128), jnp.int32),
             tiles(24), tiles(12), tiles(12), tiles(16), tiles(16),
-            tiles(8), tiles(8), tiles(4), tiles(4),
-            tiles(32), tiles(32), tiles(32),
+            tiles(8), tiles(8), tiles(4), tiles(4), tiles(4),
+            tiles(32), tiles(32),
             pltpu.SemaphoreType.DMA((SEMS,)),
             pltpu.SemaphoreType.DMA((SEMS,)),
-            pltpu.SemaphoreType.DMA((33,)),
+            pltpu.SemaphoreType.DMA((6,)),
         ],
         compiler_params=pltpu.CompilerParams(
-            collective_id=0, has_side_effects=True, vmem_limit_bytes=67043328
+            collective_id=0, has_side_effects=True, vmem_limit_bytes=VMEM_BYTES
         ),
     )(
-        tab, tab,
+        tile_coords[0, 0], tile_counts[0, 0],
         user_factors.reshape(8, 128, 256),
         item_factors.reshape(32, 128, 256),
         tile_values[0, 0],

time: 218 us -> 195 us (0.89)
  the two profiles are of different devices: /device:TPU:8 before, /device:TPU:1 now
where the time goes in v2:
time: 195 us; the launch traced here: 194 us
  Pallas kernels  191 us (98%)
  local copies, waits for them, and re-layouts  2.99 us (2%)
    pallas_call x1, Pallas kernels, per_device(): pl.pallas_call(lambda *refs: kernel(strata, *refs), out_shape=(pltpu.VMEM...  191 us

profile of v2, /device:TPU:1, one launch (start us, length us, event | category | flops | bytes accessed | tf_op | source)
XLA Modules:
  0.0 194.5 jit_solution(7281269367218469267)
XLA Ops:
  0.6 190.8 %shard_map.68 = (f32[8,128,256]{2,1,0:T(8,128)S(1)}, f32[32,128,256]{2,1,0:T(8,128)S(1)}) custom-call(s32[3,2,16]{2,1,0:T(2,128)} %bitcast.12, s32[3]{0:T(128)} %bitcast.13, f32[8,128,256]{2,1,0:T(8,128)} %bitcast.11, f32[32,128,256]{2,1,0:T(8,128)} %bitcast.9, bf16[3,16,128,128]{3,2,1,0:T(8,128)(2,1)} %bitcast.10), custom_call_target="tpu_custom_call" | custom-call | tf_op jit(solution)/shard_map/pallas_call | solution.py:658
  191.5 1.0 copy.9
  192.4 2.0 %copy.10 = f32[4096,256]{1,0:T(8,128)} copy(f32[4096,256]{1,0:T(8,128)S(1)} %bitcast.7) | data formatting | bytes 8388608
